TPU v7x, 32 devices: a whole 2x2x4 slice. The times are simulated.
32 devices in a mesh: gz: 4 (over z), gx: 2 (over x), gy: 4 (over y, core).
Axes of the slice: x: 2, y: 2, z: 4, core: 2. Of those that a mesh axis runs over, the one named last changes fastest.
Arguments:
- density: float32 [128, 256, 512], P('gx', 'gy', 'gz'), may hold values from 0.01 to 1
- design_mask: int32 [128, 256, 512], P('gx', 'gy', 'gz'), may hold values from 0 to 2
- energy: bfloat16 [4, 128, 256, 512], P(None, 'gx', 'gy', 'gz'), may hold values from 0.099609375 to 3
- decay: float32 [4, 512], P(None, 'gz'), may hold values from 0.3 to 1
- case_index: int32 [4], replicated, may hold values from 0 to 15
- case_weight: float32 [16], replicated, may hold values from 0.2 to 1
Outputs:
- sensitivity: float32 [128, 256, 512], P('gx', 'gy', 'gz')
- compliance: float32 [4], replicated
All inputs are finite; a program needn't handle non-finite values.
Results may differ from a plain program's by a relative error of at most 0.0006.
Values may be sent and summed in bfloat16 or wider, within the bound.
No kernel may reach another device: no remote copies, remote signals or barrier semaphores. Data moves between devices by JAX's collectives and lax.ppermute only.
A program may use at most 128 MiB of HBM per device.

v0:
```python
import jax
import jax.numpy as jnp
from jax import lax
from jax.sharding import PartitionSpec as P

LOADS = 16
RADIUS = 3


def entering_2(value, axis, join, neutral, backward):
    count, mine = (lax.axis_size(axis), lax.axis_index(axis))
    pieces = jax.tree.map(lambda part: lax.all_gather(part, axis), value)
    if backward:
        pieces = jax.tree.map(lambda part: part[::-1], pieces)
        mine = count - 1 - mine
    total = jax.tree.map(
        lambda part, zero: jnp.full_like(part, 0) + jnp.asarray(zero, part.dtype), value, neutral
    )

    def step(position, total):
        longer = join(total, jax.tree.map(lambda part: part[position], pieces))
        return jax.tree.map(lambda new, old: jnp.where(position < mine, new, old), longer, total)

    return lax.fori_loop(0, count - 1, step, total)


def with_halo(shard, sides, width):
    for axis, dim in sides:
        devices, length = (lax.axis_size(axis), shard.shape[dim])
        up = [(i, (i + 1) % devices) for i in range(devices - 1)]
        down = [(j, i) for i, j in up]
        last = lax.slice_in_dim(shard, length - width, length, axis=dim)
        initial = lax.slice_in_dim(shard, 0, width, axis=dim)
        before = lax.ppermute(last, axis, up)
        after = lax.ppermute(initial, axis, down)
        shard = jnp.concatenate([before, shard, after], axis=dim)
    return shard


def kernel_taps():
    offsets = jnp.arange(-RADIUS, RADIUS + 1).astype(jnp.float32)
    raw_taps = jnp.exp(-2.0 * offsets * offsets / (RADIUS * RADIUS))
    return raw_taps / jnp.sum(raw_taps)


def planar_filter(padded):
    width_x = padded.shape[1] - 2 * RADIUS
    width_y = padded.shape[2] - 2 * RADIUS
    taps = kernel_taps()
    along_x = taps[0] * padded[:, 0:width_x]
    for offset in range(1, 2 * RADIUS + 1):
        along_x = along_x + taps[offset] * padded[:, offset : offset + width_x]
    along_y = taps[0] * along_x[:, :, 0:width_y]
    for offset in range(1, 2 * RADIUS + 1):
        along_y = along_y + taps[offset] * along_x[:, :, offset : offset + width_y]
    return along_y


def solid_density(density, design_mask):
    return jnp.where(design_mask == 1, 0.001, jnp.where(design_mask == 2, 1.0, density))


def chain_maps(earlier, later):
    return (earlier[0] * later[0], later[0] * earlier[1] + later[1])


def slab_smooth(field, decay):
    depth = decay.shape[1]
    logs = jnp.log(decay)
    row_index = jnp.arange(depth)[:, None]
    col_index = jnp.arange(depth)[None, :]
    below_mask = (row_index >= col_index)[None]
    above_mask = (row_index <= col_index)[None]
    keep_in = (1.0 - decay)[:, None, :]
    upward = jnp.cumsum(logs, axis=1)
    spread = upward[:, :, None] - upward[:, None, :]
    forward_map = jnp.where(below_mask, jnp.exp(jnp.where(below_mask, spread, 0.0)), 0.0) * keep_in
    local_forward = jnp.einsum(
        "cxyj,cij->cxyi", field, forward_map, precision=lax.Precision.HIGHEST
    )
    leading = jnp.exp(upward)
    ones_part = jnp.ones((field.shape[0], 1, 1), jnp.float32)
    zero_part = jnp.zeros(field.shape[:3], jnp.float32)
    _, entering = entering_2(
        (leading[:, -1][:, None, None], local_forward[..., -1]),
        "gz",
        chain_maps,
        (ones_part, zero_part),
        False,
    )
    forward = local_forward + leading[:, None, None, :] * entering[..., None]
    remain = jnp.cumsum(logs[:, ::-1], axis=1)[:, ::-1]
    spread_back = remain[:, :, None] - remain[:, None, :]
    backward_map = (
        jnp.where(above_mask, jnp.exp(jnp.where(above_mask, spread_back, 0.0)), 0.0) * keep_in
    )
    local_backward = jnp.einsum(
        "cxyj,cij->cxyi", forward, backward_map, precision=lax.Precision.HIGHEST
    )
    trailing = jnp.exp(remain)
    _, from_above = entering_2(
        (trailing[:, 0][:, None, None], local_backward[..., 0]),
        "gz",
        chain_maps,
        (ones_part, zero_part),
        True,
    )
    return local_backward + trailing[:, None, None, :] * from_above[..., None]


def shards(density, design_mask, energy, decay, case_index, case_weight):
    dense = solid_density(density, design_mask)
    energy_wide = energy.astype(jnp.float32)
    source = -3.0 * (dense**3)[None] * energy_wide
    along_z = slab_smooth(source, decay)
    padded = with_halo(along_z.astype(jnp.bfloat16), (("gx", 1), ("gy", 2)), RADIUS).astype(
        along_z.dtype
    )
    smooth = planar_filter(padded)
    filtered = smooth / jnp.maximum(dense, 0.1)[None]
    selector = (case_index[:, None] == jnp.arange(LOADS)[None, :]).astype(jnp.float32)
    weights = jnp.sum(selector * case_weight[None, :], axis=1)
    combined = jnp.sum(weights[:, None, None, None] * filtered, axis=0)
    sensitivity = jnp.where(design_mask == 0, combined, 0.0).astype(jnp.float32)
    partial_sums = jnp.sum((dense**3)[None] * energy_wide, axis=(1, 2, 3))
    totals = lax.psum(partial_sums, ("gz", "gx", "gy"))
    all_cells = (
        density.shape[0]
        * density.shape[1]
        * density.shape[2]
        * lax.axis_size("gz")
        * lax.axis_size("gx")
        * lax.axis_size("gy")
    )
    return (sensitivity, totals / all_cells)


def solution(mesh):
    placed = (
        P("gx", "gy", "gz"),
        P("gx", "gy", "gz"),
        P(None, "gx", "gy", "gz"),
        P(None, "gz"),
        P(),
        P(),
    )
    return jax.shard_map(
        shards, mesh=mesh, in_specs=placed, out_specs=(P("gx", "gy", "gz"), P()), check_vma=False
    )
```

profile of v0, /device:TPU:1, one launch (start us, length us, event | category | flops | bytes accessed | tf_op | source)
XLA Modules:
  0.0 231.6 jit_solution(8170152929128144087)
XLA Ops:
  4.9 10.7 %all-reduce.2 = (f32[16]{0:T(128)S(1)}, f32[16]{0:T(128)S(1)}) all-reduce(f32[16]{0:T(128)S(1)} %dynamic-update-slice, f32[16]{0:T(128)S(1)} %dynamic-update-slice.1), channel_id=2, replica_groups=mesh['gz'=4,'gx'=2,'gy'=4] {'gz'}, use_global_device_ids=true, to_apply=%add | all-reduce | flops 32 | bytes 256
  15.8 4.5 %broadcast_multiply_fusion = (f32[64,64,128]{2,1,0:T(8,128)S(1)}, f32[64,64,128]{2,1,0:T(8,128)}, f32[64,64,128]{2,1,0:T(8,128)S(1)}) fusion(f32[64,64,128]{2,1,0:T(8,128)} %param.10, s32[64,64,128]{2,1,0:T(8,128)} %param.11), kind=kLoop, calls=%fused_computation.51 | loop fusion | flops 4194304 | bytes 10485760 | tf_op jit(solution)/shard_map/mul | solution.py:114
  20.3 8.6 %fusion.8 = f32[4,64,64,128]{3,2,1,0:T(8,128)S(1)} fusion(bf16[4,64,64,128]{3,2,1,0:T(8,128)(2,1)S(1)} %copy-done.2, f32[64,64,128]{2,1,0:T(8,128)S(1)} %get-tuple-element.290, f32[4,128]{1,0:T(4,128)S(1)} %get-tuple-element.298, f32[4,128]{1,0:T(4,128)S(1)} %reduce_window_sum.17, pred[128,128]{1,0:T(8,128)(4,1)S(1)} %iota_compare_fusion.1), kind=kOutput, calls=%fused_computation.21 | convolution fusion | flops 3225681920 | bytes 14700544 | tf_op jit(solution)/shard_map/cxyj,cij->cxyi/dot_general | solution.py:78
  28.9 3.2 %copy-done = f32[4,64,64,128]{3,2,1,0:T(8,128)} copy-done((f32[4,64,64,128]{3,2,1,0:T(8,128)}, f32[4,64,64,128]{3,2,1,0:T(8,128)S(1)}, u32[]{:S(2)}) %copy-start) | copy-done | bytes 8388632
  32.1 5.4 %slice.123 = f32[4,64,64,1]{3,2,1,0:T(8,128)} slice(f32[4,64,64,128]{3,2,1,0:T(8,128)S(1)} %fusion.8), slice={[0:4], [0:64], [0:64], [127:128]} | slice | bytes 131072 | tf_op jit(solution)/shard_map/slice | solution.py:85
  37.6 5.4 %copy.16 = f32[4,64,64,1]{2,1,3,0:T(8,128)S(1)} copy(f32[4,64,64,1]{3,2,1,0:T(8,128)} %slice.123) | data formatting | bytes 131072 | tf_op jit(solution)/shard_map/slice | solution.py:85
  43.0 12.8 %all-gather.1 = f32[16,64,64,1]{2,1,3,0:T(8,128)S(1)} all-gather(f32[4,64,64,1]{2,1,3,0:T(8,128)S(1)} %copy.16), channel_id=3, replica_groups=mesh['gz'=4,'gx'=2,'gy'=4] {'gz'}, dimensions={0}, use_global_device_ids=true | all-gather | bytes 327680 | tf_op jit(solution)/shard_map/all_gather | solution.py:12
  56.1 11.1 %fusion.18 = f32[4,64,64,128]{3,2,1,0:T(8,128)} fusion(f32[4,64,64,128]{3,2,1,0:T(8,128)} %copy-done, f32[4,64,64]{2,1,0:T(8,128)S(1)} %get-tuple-element.190, f32[4,128]{1,0:T(4,128)S(1)} %exp.23, f32[4,128]{1,0:T(4,128)S(1)} %rev.13, f32[4,128]{1,0:T(4,128)S(1)} %get-tuple-element.298, pred[128,128]{1,0:T(8,128)(4,1)S(1)} %iota_compare_fusion), kind=kOutput, calls=%fused_computation.39 | convolution fusion | flops 3225681920 | bytes 16865280 | tf_op jit(solution)/shard_map/cxyj,cij->cxyi/dot_general | solution.py:97
  67.2 5.4 %copy.18 = f32[4,64,64,1]{2,1,3,0:T(8,128)S(1)} copy(f32[4,64,64,1]{3,2,1,0:T(8,128)} %bitcast.43) | data formatting | bytes 131072 | tf_op jit(solution)/shard_map/slice | solution.py:102
  72.6 13.0 %all-gather.3 = f32[16,64,64,1]{2,1,3,0:T(8,128)S(1)} all-gather(f32[4,64,64,1]{2,1,3,0:T(8,128)S(1)} %copy.18), channel_id=5, replica_groups=mesh['gz'=4,'gx'=2,'gy'=4] {'gz'}, dimensions={0}, use_global_device_ids=true | all-gather | bytes 327680 | tf_op jit(solution)/shard_map/all_gather | solution.py:12
  86.1 6.0 %add_convert_fusion = bf16[4,64,64,128]{3,2,1,0:T(8,128)(2,1)S(1)} fusion(f32[4,64,64,128]{3,2,1,0:T(8,128)} %fusion.18, f32[4,64,64]{2,1,0:T(8,128)S(1)} %get-tuple-element.191, f32[4,128]{1,0:T(4,128)S(1)} %exp.25), kind=kLoop, calls=%fused_computation.38 | loop fusion | flops 6291456 | bytes 12650496 | tf_op jit(solution)/shard_map/convert_element_type | solution.py:116
  92.1 2.1 copy-done.1
  94.2 3.1 %collective-permute-start = (bf16[4,3,64,128]{3,2,1,0:T(8,128)(2,1)S(1)}, bf16[4,3,64,128]{3,2,1,0:T(8,128)(2,1)S(1)}, u32[]{:S(2)}, u32[]{:S(2)}) collective-permute-start(bf16[4,3,64,128]{3,2,1,0:T(8,128)(2,1)S(1)} %get-tuple-element.295), channel_id=1, source_target_pairs={{0,4},{1,5},{2,6},{3,7},{8,12},{9,13},{10,14},{11,15},{16,20},{17,... | collective-permute-start | bytes 589832 | tf_op jit(solution)/shard_map/ppermute | solution.py:34
  97.3 1.3 collective-permute-start.1
  99.2 1.5 fusion.9
  101.4 45.9 %psum.7 = f32[4]{0:T(128)S(1)} all-reduce(f32[4]{0:T(128)S(1)} %fusion.9), channel_id=1, replica_groups=mesh['gz'=4,'gx'=2,'gy'=4] {'gz','gx','gy'}, use_global_device_ids=true, to_apply=%region_10.11 | all-reduce | flops 4 | bytes 32 | tf_op jit(solution)/shard_map/psum | solution.py:126
  148.2 1.5 pad_maximum_fusion.2
  149.7 5.3 %collective-permute-start.2 = (bf16[4,70,3,128]{3,2,1,0:T(4,128)(2,1)S(1)}, bf16[4,70,3,128]{3,2,1,0:T(4,128)(2,1)S(1)}, u32[]{:S(2)}, u32[]{:S(2)}) collective-permute-start(bf16[4,70,3,128]{3,2,1,0:T(4,128)(2,1)S(1)} %get-tuple-element.292), channel_id=1, source_target_pairs={{0,1},{1,2},{2,3},{4,5},{5,6},{6,7},{8,9},{9,10},{10,11},{12,13},{... | collective-permute-start | bytes 645128 | tf_op jit(solution)/shard_map/ppermute | solution.py:34
  155.0 2.1 collective-permute-start.3
  158.5 4.4 %collective-permute-done.3 = bf16[4,70,3,128]{3,2,1,0:T(4,128)(2,1)S(1)} collective-permute-done((bf16[4,70,3,128]{3,2,1,0:T(4,128)(2,1)S(1)}, bf16[4,70,3,128]{3,2,1,0:T(4,128)(2,1)S(1)}, u32[]{:S(2)}, u32[]{:S(2)}) %collective-permute-start.3) | collective-permute-done | bytes 215072 | tf_op jit(solution)/shard_map/ppermute | solution.py:35
  162.9 8.4 %maximum_convert_fusion = f32[4,70,70,128]{3,2,1,0:T(8,128)} fusion(bf16[4,70,3,128]{3,2,1,0:T(4,128)(2,1)S(1)} %collective-permute-done.3, bf16[4,3,64,128]{3,2,1,0:T(8,128)(2,1)S(1)} %collective-permute-done.1, bf16[4,64,64,128]{3,2,1,0:T(8,128)(2,1)} %copy-done.1, bf16[4,3,64,128]{3,2,1,0:T(8,128)(2,1)S(1)} %collective-permute-done, ...), kind=kLoop, calls=%fused_computation.43 | loop fusion | flops 25088000 | bytes 15052800 | tf_op jit(solution)/shard_map/convert_element_type | solution.py:116
  171.3 30.3 %fusion.2 = f32[4,64,70,128]{3,2,1,0:T(8,128)} fusion(f32[4,70,70,128]{3,2,1,0:T(8,128)} %maximum_convert_fusion, f32[]{:T(128)} %bitcast.15, f32[]{:T(128)} %bitcast.14, f32[]{:T(128)} %bitcast.13, f32[]{:T(128)} %bitcast.12, f32[]{:T(128)} %bitcast.11, f32[]{:T(128)} %bitcast.10, f32[]{:T(128)} %bitcast), kind=kLoop, calls=%fused_computation.9 | loop fusion | flops 29818880 | bytes 73400352 | tf_op jit(solution)/shard_map/add | solution.py:52
  201.6 28.3 %fusion.21 = f32[64,64,128]{2,1,0:T(8,128)S(1)} fusion(f32[4,64,70,128]{3,2,1,0:T(8,128)} %fusion.2, f32[64,64,128]{2,1,0:T(8,128)S(1)} %get-tuple-element.294, f32[]{:T(128)} %bitcast.15, f32[]{:T(128)} %bitcast.14, f32[]{:T(128)} %bitcast.13, f32[]{:T(128)} %bitcast.12, f32[]{:T(128)} %bitcast.11, f32[]{:T(128)} %bitcast.10, f32[]{:T(128)} %bitcast, ...), kind=kLoop, calls=%fused_computation.42 | loop fusion | flops 33030144 | bytes 62914604 | tf_op jit(solution)/shard_map/reduce_sum | solution.py:123
  229.9 1.7 compare_select_fusion
  (59 shorter events, 8.7 us)
Async XLA Ops:
  15.8 4.5 %copy-start.2 = (bf16[4,64,64,128]{3,2,1,0:T(8,128)(2,1)S(1)}, bf16[4,64,64,128]{3,2,1,0:T(8,128)(2,1)}, u32[]{:S(2)}) copy-start(bf16[4,64,64,128]{3,2,1,0:T(8,128)(2,1)} %param.12) | copy-start | bytes 12582916
  28.9 3.2 %copy-start = (f32[4,64,64,128]{3,2,1,0:T(8,128)}, f32[4,64,64,128]{3,2,1,0:T(8,128)S(1)}, u32[]{:S(2)}) copy-start(f32[4,64,64,128]{3,2,1,0:T(8,128)S(1)} %fusion.8) | copy-start | bytes 25165828
  86.0 13.2 %copy-start.3 = (bf16[4,64,64,128]{3,2,1,0:T(8,128)(2,1)S(1)}, bf16[4,64,64,128]{3,2,1,0:T(8,128)(2,1)}, u32[]{:S(2)}) copy-start(bf16[4,64,64,128]{3,2,1,0:T(8,128)(2,1)} %param.12) | copy-start | bytes 12582916
  86.0 13.2 %copy-start.5 = (f32[64,64,128]{2,1,0:T(8,128)S(1)}, f32[64,64,128]{2,1,0:T(8,128)}, u32[]{:S(2)}) copy-start(f32[64,64,128]{2,1,0:T(8,128)} %get-tuple-element.291) | copy-start | bytes 6291460
  86.1 62.0 %copy-start.6 = (f32[16]{0:T(128)S(1)}, f32[16]{0:T(128)}, u32[]{:S(2)}) copy-start(f32[16]{0:T(128)} %param.15) | copy-start | bytes 196
  86.1 61.9 %copy-start.7 = (s32[4]{0:T(128)S(1)}, s32[4]{0:T(128)}, u32[]{:S(2)}) copy-start(s32[4]{0:T(128)} %param.14) | copy-start | bytes 52
  92.0 2.1 copy-start.1
  94.2 54.0 %collective-permute-start = (bf16[4,3,64,128]{3,2,1,0:T(8,128)(2,1)S(1)}, bf16[4,3,64,128]{3,2,1,0:T(8,128)(2,1)S(1)}, u32[]{:S(2)}, u32[]{:S(2)}) collective-permute-start(bf16[4,3,64,128]{3,2,1,0:T(8,128)(2,1)S(1)} %get-tuple-element.295), channel_id=1, source_target_pairs={{0,4},{1,5},{2,6},{3,7},{8,12},{9,13},{10,14},{11,15},{16,20},{17,... | collective-permute-start | bytes 589832 | tf_op jit(solution)/shard_map/ppermute | solution.py:34
  97.3 50.9 %collective-permute-start.1 = (bf16[4,3,64,128]{3,2,1,0:T(8,128)(2,1)S(1)}, bf16[4,3,64,128]{3,2,1,0:T(8,128)(2,1)S(1)}, u32[]{:S(2)}, u32[]{:S(2)}) collective-permute-start(bf16[4,3,64,128]{3,2,1,0:T(8,128)(2,1)S(1)} %get-tuple-element.296), channel_id=1, source_target_pairs={{4,0},{5,1},{6,2},{7,3},{12,8},{13,9},{14,10},{15,11},{20,16},{21,... | collective-permute-start | bytes 589832 | tf_op jit(solution)/shard_map/ppermute | solution.py:35
  149.7 8.8 %collective-permute-start.2 = (bf16[4,70,3,128]{3,2,1,0:T(4,128)(2,1)S(1)}, bf16[4,70,3,128]{3,2,1,0:T(4,128)(2,1)S(1)}, u32[]{:S(2)}, u32[]{:S(2)}) collective-permute-start(bf16[4,70,3,128]{3,2,1,0:T(4,128)(2,1)S(1)} %get-tuple-element.292), channel_id=1, source_target_pairs={{0,1},{1,2},{2,3},{4,5},{5,6},{6,7},{8,9},{9,10},{10,11},{12,13},{... | collective-permute-start | bytes 645128 | tf_op jit(solution)/shard_map/ppermute | solution.py:34
  155.0 8.0 %collective-permute-start.3 = (bf16[4,70,3,128]{3,2,1,0:T(4,128)(2,1)S(1)}, bf16[4,70,3,128]{3,2,1,0:T(4,128)(2,1)S(1)}, u32[]{:S(2)}, u32[]{:S(2)}) collective-permute-start(bf16[4,70,3,128]{3,2,1,0:T(4,128)(2,1)S(1)} %get-tuple-element.293), channel_id=1, source_target_pairs={{1,0},{2,1},{3,2},{5,4},{6,5},{7,6},{9,8},{10,9},{11,10},{13,12},{... | collective-permute-start | bytes 645128 | tf_op jit(solution)/shard_map/ppermute | solution.py:35
  201.6 28.3 %copy-start.4 = (s32[64,64,128]{2,1,0:T(8,128)S(1)}, s32[64,64,128]{2,1,0:T(8,128)}, u32[]{:S(2)}) copy-start(s32[64,64,128]{2,1,0:T(8,128)} %param.11) | copy-start | bytes 6291460
where the time goes:
time: 232 us
  other arithmetic  86 us (37%)
  blocking collectives  82.4 us (36%)
  local copies, waits for them, and re-layouts  24.7 us (11%)
  matrix products  19.7 us (8%)
  starting transfers between devices  11.8 us (5%)
  waiting for transfers between devices  5.3 us (2%)
    psum x1, blocking collectives, shards(): totals = lax.psum(partial_sums, ('gz', 'gx', 'gy'))  45.9 us
    add x1, other arithmetic, planar_filter(): along_x = along_x + taps[offset] * padded[:, offset:offset + width_x]  30.3 us
    reduce_sum x1, other arithmetic, shards(): combined = jnp.sum(weights[:, None, None, None] * filtered, axis=0)  28.3 us
    all_gather x2, blocking collectives, entering_2(): pieces = jax.tree.map(lambda part: lax.all_gather(part, axis), value)  25.8 us
    dot_general x1, matrix products, slab_smooth(): jnp.einsum('cxyj,cij->cxyi', forward, backward_map, precision=lax.Precisi...  11.1 us
    slice x2, local copies, waits for them, and re-layouts, slab_smooth(): local_forward[..., -1]  10.8 us
    unnamed x1, blocking collectives  10.7 us
    dot_general x1, matrix products, slab_smooth(): jnp.einsum('cxyj,cij->cxyi', field, forward_map, precision=lax.Precision....  8.58 us
  transfers between devices with their start and end apart: 4, of which 2 were waited for; matrix products, arithmetic and copies ran while one was open for 2% of the time, Pallas kernels for 0%

commit v1 on v0

--- a/solution.py
+++ b/solution.py
@@ -123,7 +123,8 @@
     combined = jnp.sum(weights[:, None, None, None] * filtered, axis=0)
     sensitivity = jnp.where(design_mask == 0, combined, 0.0).astype(jnp.float32)
     partial_sums = jnp.sum((dense**3)[None] * energy_wide, axis=(1, 2, 3))
-    totals = lax.psum(partial_sums, ("gz", "gx", "gy"))
+    partial = lax.psum(partial_sums, ("gx", "gy"))
+    totals = lax.psum(partial, "gz")
     all_cells = (
         density.shape[0]
         * density.shape[1]

time: 232 us -> 203 us (0.88)
  blocking collectives: 82.4 us -> 48.5 us
  starting transfers between devices: 11.8 us -> 17.8 us
  other arithmetic: 86 us -> 82.5 us
  waiting for transfers between devices: 5.3 us -> 8.48 us
  local copies, waits for them, and re-layouts: 24.7 us -> 22.1 us
    psum x1, blocking collectives: 45.9 us -> 12.5 us  [shards(): partial = lax.psum(partial_sums, ('gx', 'gy'))]
    ppermute x2, starting transfers between devices: 8.39 us -> 14.5 us  [with_halo(): before = lax.ppermute(last, axis, up)]
    ppermute x2, waiting for transfers between devices: 4.4 us -> 7.36 us  [with_halo(): after = lax.ppermute(initial, axis, down)]
    unnamed x21 -> x19, local copies, waits for them, and re-layouts: 7 us -> 4.34 us
  transfers between devices with their start and end apart: 4 -> 4, of which waited for: 2 -> 3; matrix products, arithmetic and copies ran while one was open for 2% -> 1% of each run, Pallas kernels for 0% -> 0%
where the time goes in v1:
time: 203 us
  other arithmetic  82.5 us (41%)
  blocking collectives  48.5 us (24%)
  local copies, waits for them, and re-layouts  22.1 us (11%)
  matrix products  21.9 us (11%)
  starting transfers between devices  17.8 us (9%)
  waiting for transfers between devices  8.48 us (4%)
    add x1, other arithmetic, planar_filter(): along_x = along_x + taps[offset] * padded[:, offset:offset + width_x]  30.4 us
    reduce_sum x1, other arithmetic, shards(): combined = jnp.sum(weights[:, None, None, None] * filtered, axis=0)  28.3 us
    all_gather x2, blocking collectives, entering_2(): pieces = jax.tree.map(lambda part: lax.all_gather(part, axis), value)  25.8 us
    ppermute x2, starting transfers between devices, with_halo(): before = lax.ppermute(last, axis, up)  14.5 us
    psum x1, blocking collectives, shards(): partial = lax.psum(partial_sums, ('gx', 'gy'))  12.5 us
    dot_general x1, matrix products, slab_smooth(): jnp.einsum('cxyj,cij->cxyi', forward, backward_map, precision=lax.Precisi...  11.1 us
    slice x2, local copies, waits for them, and re-layouts, slab_smooth(): local_forward[..., -1]  10.8 us
    dot_general x1, matrix products, slab_smooth(): jnp.einsum('cxyj,cij->cxyi', field, forward_map, precision=lax.Precision....  10.8 us
  transfers between devices with their start and end apart: 4, of which 3 were waited for; matrix products, arithmetic and copies ran while one was open for 1% of the time, Pallas kernels for 0%

profile of v1, /device:TPU:1, one launch (start us, length us, event | category | flops | bytes accessed | tf_op | source)
XLA Modules:
  0.0 202.8 jit_solution(7798142580830456169)
XLA Ops:
  2.6 4.5 %broadcast_multiply_fusion = (f32[64,64,128]{2,1,0:T(8,128)S(1)}, f32[64,64,128]{2,1,0:T(8,128)S(1)}, f32[64,64,128]{2,1,0:T(8,128)}) fusion(f32[64,64,128]{2,1,0:T(8,128)} %param.10, s32[64,64,128]{2,1,0:T(8,128)} %param.11), kind=kLoop, calls=%fused_computation.51 | loop fusion | flops 4194304 | bytes 10485760 | tf_op jit(solution)/shard_map/mul | solution.py:114
  7.0 1.5 fusion.9
  8.5 12.5 %psum.14 = f32[4]{0:T(128)S(1)} all-reduce(f32[4]{0:T(128)S(1)} %fusion.9), channel_id=1, replica_groups=mesh['gz'=4,'gx'=2,'gy'=4] {'gx','gy'}, use_global_device_ids=true, to_apply=%region_10.11 | all-reduce | flops 4 | bytes 32 | tf_op jit(solution)/shard_map/psum | solution.py:126
  22.9 10.2 %all-reduce.2 = (f32[16]{0:T(128)S(1)}, f32[16]{0:T(128)S(1)}, f32[4]{0:T(128)S(1)}) all-reduce(f32[16]{0:T(128)S(1)} %dynamic-update-slice, f32[16]{0:T(128)S(1)} %dynamic-update-slice.1, f32[4]{0:T(128)S(1)} %psum.14), channel_id=2, replica_groups=mesh['gz'=4,'gx'=2,'gy'=4] {'gz'}, use_global_device_ids=true, to_apply=%add | all-reduce | flops 36 | bytes 288
  33.2 10.8 %fusion.8 = f32[4,64,64,128]{3,2,1,0:T(8,128)S(1)} fusion(bf16[4,64,64,128]{3,2,1,0:T(8,128)(2,1)} %param.12, f32[64,64,128]{2,1,0:T(8,128)S(1)} %get-tuple-element.291, f32[4,128]{1,0:T(4,128)S(1)} %get-tuple-element.299, f32[4,128]{1,0:T(4,128)S(1)} %reduce_window_sum.17, pred[128,128]{1,0:T(8,128)(4,1)S(1)} %iota_compare_fusion.1), kind=kOutput, calls=%fused_computation.21 | convolution fusion | flops 3225681920 | bytes 14700544 | tf_op jit(solution)/shard_map/cxyj,cij->cxyi/dot_general | solution.py:78
  44.0 3.2 %copy-done = f32[4,64,64,128]{3,2,1,0:T(8,128)} copy-done((f32[4,64,64,128]{3,2,1,0:T(8,128)}, f32[4,64,64,128]{3,2,1,0:T(8,128)S(1)}, u32[]{:S(2)}) %copy-start) | copy-done | bytes 8388632
  47.2 5.4 %slice.123 = f32[4,64,64,1]{3,2,1,0:T(8,128)} slice(f32[4,64,64,128]{3,2,1,0:T(8,128)S(1)} %fusion.8), slice={[0:4], [0:64], [0:64], [127:128]} | slice | bytes 131072 | tf_op jit(solution)/shard_map/slice | solution.py:85
  52.6 5.4 %copy.16 = f32[4,64,64,1]{2,1,3,0:T(8,128)S(1)} copy(f32[4,64,64,1]{3,2,1,0:T(8,128)} %slice.123) | data formatting | bytes 131072 | tf_op jit(solution)/shard_map/slice | solution.py:85
  58.0 13.6 %all-gather.1 = f32[16,64,64,1]{2,1,3,0:T(8,128)S(1)} all-gather(f32[4,64,64,1]{2,1,3,0:T(8,128)S(1)} %copy.16), channel_id=3, replica_groups=mesh['gz'=4,'gx'=2,'gy'=4] {'gz'}, dimensions={0}, use_global_device_ids=true | all-gather | bytes 327680 | tf_op jit(solution)/shard_map/all_gather | solution.py:12
  71.9 11.1 %fusion.18 = f32[4,64,64,128]{3,2,1,0:T(8,128)} fusion(f32[4,64,64,128]{3,2,1,0:T(8,128)} %copy-done, f32[4,64,64]{2,1,0:T(8,128)S(1)} %get-tuple-element.190, f32[4,128]{1,0:T(4,128)S(1)} %exp.23, f32[4,128]{1,0:T(4,128)S(1)} %rev.13, f32[4,128]{1,0:T(4,128)S(1)} %get-tuple-element.299, pred[128,128]{1,0:T(8,128)(4,1)S(1)} %iota_compare_fusion), kind=kOutput, calls=%fused_computation.39 | convolution fusion | flops 3225681920 | bytes 16865280 | tf_op jit(solution)/shard_map/cxyj,cij->cxyi/dot_general | solution.py:97
  83.0 5.4 %copy.18 = f32[4,64,64,1]{2,1,3,0:T(8,128)S(1)} copy(f32[4,64,64,1]{3,2,1,0:T(8,128)} %bitcast.43) | data formatting | bytes 131072 | tf_op jit(solution)/shard_map/slice | solution.py:102
  88.4 12.2 %all-gather.3 = f32[16,64,64,1]{2,1,3,0:T(8,128)S(1)} all-gather(f32[4,64,64,1]{2,1,3,0:T(8,128)S(1)} %copy.18), channel_id=5, replica_groups=mesh['gz'=4,'gx'=2,'gy'=4] {'gz'}, dimensions={0}, use_global_device_ids=true | all-gather | bytes 327680 | tf_op jit(solution)/shard_map/all_gather | solution.py:12
  101.1 5.2 %add_convert_fusion = bf16[4,64,64,128]{3,2,1,0:T(8,128)(2,1)S(1)} fusion(f32[4,64,64,128]{3,2,1,0:T(8,128)} %fusion.18, f32[4,64,64]{2,1,0:T(8,128)S(1)} %get-tuple-element.191, f32[4,128]{1,0:T(4,128)S(1)} %exp.25), kind=kLoop, calls=%fused_computation.38 | loop fusion | flops 6291456 | bytes 12650496 | tf_op jit(solution)/shard_map/convert_element_type | solution.py:116
  106.4 4.1 %collective-permute-start = (bf16[4,3,64,128]{3,2,1,0:T(8,128)(2,1)S(1)}, bf16[4,3,64,128]{3,2,1,0:T(8,128)(2,1)S(1)}, u32[]{:S(2)}, u32[]{:S(2)}) collective-permute-start(bf16[4,3,64,128]{3,2,1,0:T(8,128)(2,1)S(1)} %get-tuple-element.296), channel_id=1, source_target_pairs={{0,4},{1,5},{2,6},{3,7},{8,12},{9,13},{10,14},{11,15},{16,20},{17,... | collective-permute-start | bytes 589832 | tf_op jit(solution)/shard_map/ppermute | solution.py:34
  110.5 1.3 collective-permute-start.1
  113.9 3.0 %collective-permute-done.1 = bf16[4,3,64,128]{3,2,1,0:T(8,128)(2,1)S(1)} collective-permute-done((bf16[4,3,64,128]{3,2,1,0:T(8,128)(2,1)S(1)}, bf16[4,3,64,128]{3,2,1,0:T(8,128)(2,1)S(1)}, u32[]{:S(2)}, u32[]{:S(2)}) %collective-permute-start.1) | collective-permute-done | bytes 196640 | tf_op jit(solution)/shard_map/ppermute | solution.py:35
  117.1 10.5 %collective-permute-start.2 = (bf16[4,70,3,128]{3,2,1,0:T(4,128)(2,1)S(1)}, bf16[4,70,3,128]{3,2,1,0:T(4,128)(2,1)S(1)}, u32[]{:S(2)}, u32[]{:S(2)}) collective-permute-start(bf16[4,70,3,128]{3,2,1,0:T(4,128)(2,1)S(1)} %get-tuple-element.293), channel_id=1, source_target_pairs={{0,1},{1,2},{2,3},{4,5},{5,6},{6,7},{8,9},{9,10},{10,11},{12,13},{... | collective-permute-start | bytes 645128 | tf_op jit(solution)/shard_map/ppermute | solution.py:34
  127.6 1.9 collective-permute-start.3
  130.0 1.1 collective-permute-done.2
  131.2 4.4 %collective-permute-done.3 = bf16[4,70,3,128]{3,2,1,0:T(4,128)(2,1)S(1)} collective-permute-done((bf16[4,70,3,128]{3,2,1,0:T(4,128)(2,1)S(1)}, bf16[4,70,3,128]{3,2,1,0:T(4,128)(2,1)S(1)}, u32[]{:S(2)}, u32[]{:S(2)}) %collective-permute-start.3) | collective-permute-done | bytes 215072 | tf_op jit(solution)/shard_map/ppermute | solution.py:35
  135.5 6.8 %maximum_convert_fusion = f32[4,70,70,128]{3,2,1,0:T(8,128)} fusion(bf16[4,70,3,128]{3,2,1,0:T(4,128)(2,1)S(1)} %collective-permute-done.3, bf16[4,3,64,128]{3,2,1,0:T(8,128)(2,1)S(1)} %collective-permute-done.1, bf16[4,64,64,128]{3,2,1,0:T(8,128)(2,1)S(1)} %add_convert_fusion, bf16[4,3,64,128]{3,2,1,0:T(8,128)(2,1)S(1)} %collective-permute-done, ...), kind=kLoop, calls=%fused_computation.43 | loop fusion | flops 25088000 | bytes 15052800 | tf_op jit(solution)/shard_map/convert_element_type | solution.py:116
  142.4 30.4 %fusion.2 = f32[4,64,70,128]{3,2,1,0:T(8,128)} fusion(f32[4,70,70,128]{3,2,1,0:T(8,128)} %maximum_convert_fusion, f32[]{:T(128)} %bitcast.15, f32[]{:T(128)} %bitcast.14, f32[]{:T(128)} %bitcast.13, f32[]{:T(128)} %bitcast.12, f32[]{:T(128)} %bitcast.11, f32[]{:T(128)} %bitcast.10, f32[]{:T(128)} %bitcast), kind=kLoop, calls=%fused_computation.9 | loop fusion | flops 29818880 | bytes 73400352 | tf_op jit(solution)/shard_map/add | solution.py:52
  172.8 28.3 %fusion.21 = f32[64,64,128]{2,1,0:T(8,128)S(1)} fusion(f32[4,64,70,128]{3,2,1,0:T(8,128)} %fusion.2, f32[64,64,128]{2,1,0:T(8,128)S(1)} %copy-done.3, f32[]{:T(128)} %bitcast.15, f32[]{:T(128)} %bitcast.14, f32[]{:T(128)} %bitcast.13, f32[]{:T(128)} %bitcast.12, f32[]{:T(128)} %bitcast.11, f32[]{:T(128)} %bitcast.10, f32[]{:T(128)} %bitcast, ...), kind=kLoop, calls=%fused_computation.42 | loop fusion | flops 33030144 | bytes 62914604 | tf_op jit(solution)/shard_map/reduce_sum | solution.py:123
  201.1 1.7 compare_select_fusion
  (57 shorter events, 7.4 us)
Async XLA Ops:
  2.5 4.5 %copy-start.1 = (bf16[4,64,64,128]{3,2,1,0:T(8,128)(2,1)S(1)}, bf16[4,64,64,128]{3,2,1,0:T(8,128)(2,1)}, u32[]{:S(2)}) copy-start(bf16[4,64,64,128]{3,2,1,0:T(8,128)(2,1)} %param.12) | copy-start | bytes 12582916
  2.5 18.6 %copy-start.6 = (u32[32]{0:T(128)S(1)}, u32[32]{0:T(128)}, u32[]{:S(2)}) copy-start(u32[32]{0:T(128)} %constant.87) | copy-start | bytes 388
  43.9 3.2 %copy-start = (f32[4,64,64,128]{3,2,1,0:T(8,128)}, f32[4,64,64,128]{3,2,1,0:T(8,128)S(1)}, u32[]{:S(2)}) copy-start(f32[4,64,64,128]{3,2,1,0:T(8,128)S(1)} %fusion.8) | copy-start | bytes 25165828
  100.6 13.1 %copy-start.4 = (f32[16]{0:T(128)S(1)}, f32[16]{0:T(128)}, u32[]{:S(2)}) copy-start(f32[16]{0:T(128)} %param.15) | copy-start | bytes 196
  100.6 13.1 %copy-start.5 = (s32[4]{0:T(128)S(1)}, s32[4]{0:T(128)}, u32[]{:S(2)}) copy-start(s32[4]{0:T(128)} %param.14) | copy-start | bytes 52
  106.4 7.5 %collective-permute-start = (bf16[4,3,64,128]{3,2,1,0:T(8,128)(2,1)S(1)}, bf16[4,3,64,128]{3,2,1,0:T(8,128)(2,1)S(1)}, u32[]{:S(2)}, u32[]{:S(2)}) collective-permute-start(bf16[4,3,64,128]{3,2,1,0:T(8,128)(2,1)S(1)} %get-tuple-element.296), channel_id=1, source_target_pairs={{0,4},{1,5},{2,6},{3,7},{8,12},{9,13},{10,14},{11,15},{16,20},{17,... | collective-permute-start | bytes 589832 | tf_op jit(solution)/shard_map/ppermute | solution.py:34
  110.5 6.4 %collective-permute-start.1 = (bf16[4,3,64,128]{3,2,1,0:T(8,128)(2,1)S(1)}, bf16[4,3,64,128]{3,2,1,0:T(8,128)(2,1)S(1)}, u32[]{:S(2)}, u32[]{:S(2)}) collective-permute-start(bf16[4,3,64,128]{3,2,1,0:T(8,128)(2,1)S(1)} %get-tuple-element.297), channel_id=1, source_target_pairs={{4,0},{5,1},{6,2},{7,3},{12,8},{13,9},{14,10},{15,11},{20,16},{21,... | collective-permute-start | bytes 589832 | tf_op jit(solution)/shard_map/ppermute | solution.py:35
  117.1 14.0 %collective-permute-start.2 = (bf16[4,70,3,128]{3,2,1,0:T(4,128)(2,1)S(1)}, bf16[4,70,3,128]{3,2,1,0:T(4,128)(2,1)S(1)}, u32[]{:S(2)}, u32[]{:S(2)}) collective-permute-start(bf16[4,70,3,128]{3,2,1,0:T(4,128)(2,1)S(1)} %get-tuple-element.293), channel_id=1, source_target_pairs={{0,1},{1,2},{2,3},{4,5},{5,6},{6,7},{8,9},{9,10},{10,11},{12,13},{... | collective-permute-start | bytes 645128 | tf_op jit(solution)/shard_map/ppermute | solution.py:34
  127.6 8.0 %collective-permute-start.3 = (bf16[4,70,3,128]{3,2,1,0:T(4,128)(2,1)S(1)}, bf16[4,70,3,128]{3,2,1,0:T(4,128)(2,1)S(1)}, u32[]{:S(2)}, u32[]{:S(2)}) collective-permute-start(bf16[4,70,3,128]{3,2,1,0:T(4,128)(2,1)S(1)} %get-tuple-element.294), channel_id=1, source_target_pairs={{1,0},{2,1},{3,2},{5,4},{6,5},{7,6},{9,8},{10,9},{11,10},{13,12},{... | collective-permute-start | bytes 645128 | tf_op jit(solution)/shard_map/ppermute | solution.py:35
  142.4 30.4 %copy-start.3 = (f32[64,64,128]{2,1,0:T(8,128)S(1)}, f32[64,64,128]{2,1,0:T(8,128)}, u32[]{:S(2)}) copy-start(f32[64,64,128]{2,1,0:T(8,128)} %get-tuple-element.295) | copy-start | bytes 6291460
  172.8 28.3 %copy-start.2 = (s32[64,64,128]{2,1,0:T(8,128)S(1)}, s32[64,64,128]{2,1,0:T(8,128)}, u32[]{:S(2)}) copy-start(s32[64,64,128]{2,1,0:T(8,128)} %param.11) | copy-start | bytes 6291460
